TPU v7x, 512 devices: a whole 4x4x16 slice. The times are simulated.
512 devices in a mesh: pix: 128 (over z_hi, x, y, core), row: 4 (over z_lo).
Axes of the slice: x: 4, y: 4, z: 16 (z_hi: 4, z_lo: 4; z = z_hi * 4 + z_lo), core: 2. Of those that a mesh axis runs over, the one named last changes fastest.
Arguments:
- band_images: bfloat16 [256, 128, 8192], P('pix', 'row'), may hold values from -6 to 6
- pivots: int32 [2, 32], replicated, may hold values from 0 to 1048575, as said below
Outputs:
- residual: bfloat16 [8192, 128, 256], P(('pix', 'row'))
- coefficients: bfloat16 [64, 8192, 128], P(None, ('pix', 'row'))
Inputs may be any that keep to these rules, and one draw needn't show every extreme that they name: All 64 pivots lie in different columns, and every group of 32 lines starting at a multiple of 32 holds at least one pivot.
All inputs are finite; a program needn't handle non-finite values.
Results may differ from a plain program's by a relative error of at most 0.001.
Values may be sent and summed in bfloat16 or wider, within the bound.
A program may use at most 192 MiB of HBM per device.

v0:
```python
import jax
import jax.numpy as jnp
from jax import lax
from jax.sharding import PartitionSpec as P

highest = lax.Precision.HIGHEST


def orthonormal(spectra):
    gram = jnp.dot(spectra, spectra.T, precision=highest)
    factor = jnp.linalg.cholesky(gram)
    return jax.scipy.linalg.solve_triangular(factor, spectra, lower=True)


def project(block, basis):
    count = basis.shape[0] // 2
    first = basis[:count]
    second = basis[count:]
    coef_one = jnp.einsum("clb,kb->kcl", block, first, precision=highest)
    remain = block - jnp.einsum("kcl,kb->clb", coef_one, first, precision=highest)
    coef_two = jnp.einsum("clb,kb->kcl", remain, second, precision=highest)
    remain = remain - jnp.einsum("kcl,kb->clb", coef_two, second, precision=highest)
    return (
        remain.astype(jnp.bfloat16),
        jnp.concatenate([coef_one, coef_two], axis=0).astype(jnp.bfloat16),
    )


def shards(band_images, pivots):
    band_dev, line_dev, cols_all = band_images.shape
    pix_count = lax.axis_size("pix")
    row_count = lax.axis_size("row")
    narrow = cols_all // (pix_count * row_count)
    flat_pivots = pivots.reshape(-1)
    line_index = flat_pivots // cols_all
    column = flat_pivots % cols_all
    offset = line_index - lax.axis_index("row") * line_dev
    inside = (offset >= 0) & (offset < line_dev)
    position = jnp.clip(offset, 0, line_dev - 1) * cols_all + column
    picked = jnp.take(band_images.reshape(band_dev, line_dev * cols_all), position, axis=1)
    picked = jnp.where(inside[None, :], picked, jnp.zeros_like(picked))
    placed = jnp.zeros((band_dev * pix_count, flat_pivots.shape[0]), jnp.float32)
    placed = lax.dynamic_update_slice_in_dim(
        placed, picked.astype(jnp.float32), lax.axis_index("pix") * band_dev, 0
    )
    spectra = lax.psum(placed, ("pix", "row"))
    basis = orthonormal(spectra.T)
    shaped = band_images.reshape(band_dev, line_dev, pix_count, row_count, narrow)
    arrived = lax.all_to_all(
        lax.all_to_all(shaped, "pix", split_axis=2, concat_axis=0, tiled=True),
        "row",
        split_axis=3,
        concat_axis=1,
        tiled=True,
    )
    block = (
        arrived.reshape(arrived.shape[0], arrived.shape[1], narrow)
        .transpose(2, 1, 0)
        .astype(jnp.float32)
    )
    return project(block, basis)


def solution(mesh):
    placed = (P("pix", "row", None), P())
    return jax.shard_map(
        shards,
        mesh=mesh,
        in_specs=placed,
        out_specs=(P(("pix", "row"), None, None), P(None, ("pix", "row"), None)),
        check_vma=False,
    )
```

profile of v0, /device:TPU:1, one launch (start us, length us, event | category | flops | bytes accessed | tf_op | source)
XLA Modules:
  0.0 625.4 jit_solution(1769854623598273289)
XLA Ops:
  7.2 4.6 copy.14
  11.7 5.6 copy.22
  17.3 6.5 %reshape.198 = bf16[128,2,2048]{2,1,0:T(2,128)(2,1)S(1)} reshape(bf16[128,2,4,16,32]{4,3,2,1,0:T(8,128)(2,1)} %bitcast.50) | data formatting | bytes 2097152
  23.8 76.3 %all_to_all.33 = bf16[128,2,2048]{2,1,0:T(2,128)(2,1)S(1)} all-to-all(bf16[128,2,2048]{2,1,0:T(2,128)(2,1)S(1)} %reshape.198), channel_id=1, replica_groups=mesh['pix'=128,'row'=4] {'pix'}, dimensions={0} | all-to-all | bytes 2097152 | tf_op jit(solution)/shard_map/all_to_all | solution.py:50
  100.1 3.5 reshape.199
  103.6 6.9 %copy.16 = bf16[256,32,1,4,16]{0,4,2,1,3:T(8,128)(2,1)} copy(bf16[256,32,1,4,16]{1,4,3,0,2:T(8,128)(2,1)} %bitcast.49) | data formatting | bytes 2097152 | tf_op jit(solution)/shard_map/all_to_all | solution.py:50
  110.6 8.3 %all-to-all-start.1 = ((bf16[256,32,1,4,16]{0,4,2,1,3:T(8,128)(2,1)}), bf16[256,32,1,4,16]{0,4,2,1,3:T(8,128)(2,1)S(1)}, u32[]{:S(2)}, u32[]{:S(2)}) async-start(bf16[256,32,1,4,16]{0,4,2,1,3:T(8,128)(2,1)} %copy.16), calls=%async_computation.1 | async-start | bytes 2097152 | tf_op jit(solution)/shard_map/all_to_all | solution.py:49
  118.8 0.0 all-reduce.2.cloned.1.call-start
  118.8 0.1 reshape.185
  118.9 0.1 reshape.187
  119.0 40.3 %copy.18 = bf16[2,32,8192]{0,2,1:T(8,128)(2,1)} copy(bf16[2,32,8192]{2,1,0:T(8,128)(2,1)S(1)} %copy-done) | data formatting | bytes 2097152 | tf_op args[0]
  159.4 1.5 gather_fusion
  160.9 0.1 convert_bitcast_fusion
  161.0 0.6 dynamic_update_slice.3
  161.6 0.0 copy-start.1
  161.6 0.6 copy-done.1
  162.3 0.0 all-reduce.2.cloned.1.call-update
  162.3 432.9 %all-reduce.2.cloned.1.call-done = f32[256,64]{0,1:T(8,128)} async-done(((f32[256,64]{0,1:T(8,128)}), f32[256,64]{0,1:T(8,128)}) %all-reduce.2.cloned.1.call-update) | async-done | bytes 65552 | tf_op jit(solution)/shard_map/psum | solution.py:46
  595.2 1.1 fusion.13
  596.3 0.1 copy.19
  596.4 5.8 cholesky.16
  602.3 0.6 compare_reduce_fusion
  603.0 0.7 fusion
  603.6 4.9 custom-call.7
  608.5 1.1 fusion.1
  609.6 0.0 all-to-all-done.1
  609.6 0.3 copy.17
  610.0 1.0 fusion.12
  611.0 1.8 convert_subtract_fusion
  612.8 2.0 fusion.11
  614.9 0.9 copy.20
  615.8 2.8 subtract_convert_fusion
  (12 shorter events, 0.1 us)
Async XLA Ops:
  110.6 8.3 %copy-start.2 = (s32[2,32]{1,0:T(2,128)S(1)}, s32[2,32]{1,0:T(2,128)}, u32[]{:S(2)}) copy-start(s32[2,32]{1,0:T(2,128)} %param.3) | copy-start | bytes 772
  110.6 8.4 %copy-start = (bf16[2,32,8192]{2,1,0:T(8,128)(2,1)S(1)}, bf16[2,32,8192]{2,1,0:T(8,128)(2,1)}, u32[]{:S(2)}) copy-start(bf16[2,32,8192]{2,1,0:T(8,128)(2,1)} %param.2) | copy-start | bytes 3145732
  110.6 499.1 %all-to-all-start.1 = ((bf16[256,32,1,4,16]{0,4,2,1,3:T(8,128)(2,1)}), bf16[256,32,1,4,16]{0,4,2,1,3:T(8,128)(2,1)S(1)}, u32[]{:S(2)}, u32[]{:S(2)}) async-start(bf16[256,32,1,4,16]{0,4,2,1,3:T(8,128)(2,1)} %copy.16), calls=%async_computation.1 | async-start | bytes 2097152 | tf_op jit(solution)/shard_map/all_to_all | solution.py:49
  118.8 476.4 %all-reduce.2.cloned.1.call-start = ((), (), s32[]{:S(2)}) async-start(), calls=%async_computation.2 | async-start | bytes 131072 | tf_op jit(solution)/shard_map/psum | solution.py:46
  161.6 0.6 copy-start.1
Sparse Core Ops, SparseCore 0:
  162.4 432.7 all-reduce.1
where the time goes:
time: 626 us; the launch traced here: 625 us
  waiting for transfers between devices  433 us (69%)
  blocking collectives  76.3 us (12%)
  local copies, waits for them, and re-layouts  71.7 us (11%)
  between operations  14.2 us (2%)
  other arithmetic  12.2 us (2%)
  matrix products  9.88 us (2%)
  starting transfers between devices  8.26 us (1%)
    psum x1, waiting for transfers between devices, shards(): spectra = lax.psum(placed, ('pix', 'row'))  433 us
    all_to_all x1, blocking collectives, shards(): lax.all_to_all(shaped, 'pix', split_axis=2, concat_axis=0, tiled=True)  76.3 us
    unnamed x11, local copies, waits for them, and re-layouts  56.5 us
  transfers between devices with their start and end apart: 2, of which 1 were waited for; matrix products, arithmetic and copies ran while one was open for 9% of the time, Pallas kernels for 0%

commit v1 on v0

v1 whole, which is shorter than its diff:
```python
import functools

import jax
import jax.numpy as jnp
from jax import lax
from jax.experimental import pallas as pl
from jax.experimental.pallas import tpu as pltpu
from jax.sharding import PartitionSpec as P

MESH = pl.DeviceIdType.MESH
HIGHEST = lax.Precision.HIGHEST
NZ = 16
NQ = 32
NPIV = 64
BANDS = 256
NCH = 8
PER = NQ // NCH
SUB = 16 // NCH


def iota(shape, dim):
    return lax.broadcasted_iota(jnp.int32, shape, dim)


def one(mask, kind=jnp.bfloat16):
    return jnp.where(mask, 1.0, 0.0).astype(kind)


def nn(a, b, precision=None):
    return jnp.dot(a, b, precision=precision, preferred_element_type=jnp.float32)


def nt(a, b, precision=None):
    return lax.dot_general(
        a, b, (((1,), (1,)), ((), ())), precision=precision, preferred_element_type=jnp.float32
    )


def tn(a, b, precision=None):
    return lax.dot_general(
        a, b, (((0,), (0,)), ((), ())), precision=precision, preferred_element_type=jnp.float32
    )


def split(w):
    high = w.astype(jnp.bfloat16)
    return high, (w - high.astype(jnp.float32)).astype(jnp.bfloat16)


def far_order(i):
    half = (i + 1) // 2
    return jnp.where(lax.rem(i, 2) == 1, 8 - half, 8 + half)


def exchange(
    a_ref, piv_ref,
    x_ref, mh_ref, ml_ref, ch_ref, cl_ref,
    sb, p1, tb, stage, perm, ps, pz, pq, rs,
    local_sem, z_send, z_recv, q_send, q_recv, pz_send, pz_recv, pq_send, pq_recv,
):
    pix = lax.axis_index("pix")
    row = lax.axis_index("row")
    q = lax.rem(pix, NQ)
    z_hi = pix // NQ
    z = z_hi * 4 + row
    own_chunk = q // PER

    def z_device(zz):
        return ((zz // 4) * NQ + q, lax.rem(zz, 4))

    def q_device(qq):
        return (z_hi * NQ + qq, row)

    barrier = pltpu.get_barrier_semaphore()

    @pl.loop(1, NZ)
    def _(d):
        pl.semaphore_signal(
            barrier, inc=1, device_id=z_device(lax.rem(z + d, NZ)), device_id_type=MESH
        )

    @pl.loop(1, NQ)
    def _(d):
        pl.semaphore_signal(
            barrier, inc=1, device_id=q_device(lax.rem(q + d, NQ)), device_id_type=MESH
        )

    r64, k256 = iota((64, 256), 0), iota((64, 256), 1)
    pick = one(
        ((r64 >> 3) == ((k256 & 127) >> 4))
        & ((r64 & 3) == ((k256 >> 2) & 3))
        & (((r64 >> 2) & 1) == (k256 >> 7))
    )
    lane = iota((32, 128), 1)
    masks = [one((lane & 3) == s) for s in range(4)]

    def chunk_at(k):
        return lax.rem(own_chunk + 1 + k, NCH)

    def relayout(ck):
        for i in range(SUB):
            for zh in range(4):
                col = pl.multiple_of((zh * 16 + ck * SUB + i) * 128, 128)
                halves = []
                for j in range(2):
                    a = a_ref[j, :, pl.ds(col, 128)]
                    halves.append(jnp.concatenate([a * m for m in masks], axis=0))
                out = nt(pick, jnp.concatenate(halves, axis=1)).astype(jnp.bfloat16)
                for m in range(8):
                    sb[ck, zh * 4 + m % 4, (i * 2 + m // 4) * 8 : (i * 2 + m // 4 + 1) * 8, :] = (
                        out[m * 8 : (m + 1) * 8, :]
                    )

    def send_z(k, ck):
        pltpu.make_async_copy(sb.at[ck, z], p1.at[k, z], local_sem.at[k]).start()

        @pl.loop(0, NZ - 1)
        def _(i):
            zz = lax.rem(z + far_order(i), NZ)
            pltpu.make_async_remote_copy(
                sb.at[ck, zz], p1.at[k, z], z_send.at[0], z_recv.at[k],
                device_id=z_device(zz), device_id_type=MESH,
            ).start()

    relayout(chunk_at(0))

    pivots = jnp.concatenate([piv_ref[0:1, :], piv_ref[1:2, :]], axis=1)
    column = pivots & 8191
    offset = (pivots >> 13) - row * 32
    picked = jnp.zeros((64, NPIV), jnp.float32)

    def pick_columns(t, acc):
        at = pl.multiple_of(t * 512, 512)
        hot = one((iota((512, NPIV), 0) + t * 512) == column)
        both = jnp.concatenate(
            [a_ref[0, :, pl.ds(at, 512)], a_ref[1, :, pl.ds(at, 512)]], axis=0
        )
        return acc + nn(both, hot)

    picked = lax.fori_loop(0, 16, pick_columns, picked)
    line = iota((32, NPIV), 0)
    here = jnp.where(line == offset, 1.0, 0.0)
    own = [
        jnp.sum(picked[j * 32 : (j + 1) * 32, :] * here, axis=0, keepdims=True) for j in range(2)
    ]
    rows8 = iota((8, NPIV), 0)
    tile = jnp.where(rows8 == 0, own[0], jnp.where(rows8 == 1, own[1], 0.0))
    ps[...] = jnp.concatenate([tile, jnp.zeros_like(tile)], axis=1).astype(jnp.bfloat16)

    pl.semaphore_wait(barrier, NZ - 1 + NQ - 1)

    pltpu.make_async_copy(ps, pz.at[z], local_sem.at[NCH]).start()

    @pl.loop(0, NZ - 1)
    def _(i):
        zz = lax.rem(z + far_order(i), NZ)
        pltpu.make_async_remote_copy(
            ps, pz.at[z], pz_send.at[0], pz_recv.at[0],
            device_id=z_device(zz), device_id_type=MESH,
        ).start()

    send_z(0, chunk_at(0))

    @pl.loop(1, NCH)
    def _(k):
        ck = chunk_at(k)
        relayout(ck)
        send_z(k, ck)

    pltpu.make_async_copy(ps, pz.at[z], local_sem.at[NCH]).wait()
    pltpu.make_async_copy(pz.at[0 : NZ - 1], pz.at[0 : NZ - 1], pz_recv.at[0]).wait()
    r8 = iota((8, 128), 0)
    plane = jnp.zeros((8, 128), jnp.float32)
    for zh in range(4):
        part = pz[zh * 4].astype(jnp.float32)
        for zl in range(1, 4):
            part = part + pz[zh * 4 + zl].astype(jnp.float32)
        for j in range(2):
            plane = jnp.where(r8 == zh * 2 + j, part[j : j + 1, :], plane)
    pq[...] = plane.astype(jnp.bfloat16)
    pltpu.make_async_copy(pq, rs.at[q], local_sem.at[NCH]).start()

    @pl.loop(1, NQ)
    def _(d):
        pltpu.make_async_remote_copy(
            pq, rs.at[q], pq_send.at[0], pq_recv.at[0],
            device_id=q_device(lax.rem(q + d, NQ)), device_id_type=MESH,
        ).start()

    for t in range(4):
        n512, k128 = iota((128, 512), 1), iota((128, 512), 0)
        perm[t * 128 : (t + 1) * 128, :] = one(
            ((k128 >> 5) == (n512 >> 7)) & (((n512 >> 5) & 3) == t) & ((k128 & 31) == (n512 & 31))
        )

    pltpu.make_async_copy(pq, rs.at[q], local_sem.at[NCH]).wait()
    pltpu.make_async_copy(rs.at[0 : NQ - 1], rs.at[0 : NQ - 1], pq_recv.at[0]).wait()

    arrived = rs[...].astype(jnp.float32).reshape(BANDS, 128).astype(jnp.bfloat16)
    eye = one(iota((NPIV, 128), 0) == iota((NPIV, 128), 1))
    spectra_in = nt(eye, arrived).astype(jnp.bfloat16)
    b_in, b_own = iota((BANDS, BANDS), 0), iota((BANDS, BANDS), 1)
    same = (((b_in >> 1) & 3) * 64 + (b_in >> 3) * 2 + (b_in & 1)) == b_own
    spectra_own = nn(spectra_in, one(same))
    gram = nt(spectra_in, spectra_in)
    sub, lan = iota((NPIV, 128), 0), iota((NPIV, 128), 1)
    wide = jnp.concatenate([gram, one(sub[:, :NPIV] == lan[:, :NPIV], jnp.float32)], axis=1)

    def eliminate(k, w):
        pivot_row = jnp.sum(jnp.where(sub == k, w, 0.0), axis=0, keepdims=True)
        pivot_col = jnp.sum(jnp.where(lan == k, w, 0.0), axis=1, keepdims=True)
        diag = jnp.sum(jnp.where(lan[:1] == k, pivot_row, 0.0), axis=1, keepdims=True)
        ratio = jnp.where(sub[:, :1] > k, pivot_col, 0.0) / diag
        return w - ratio * pivot_row

    wide = lax.fori_loop(0, NPIV, eliminate, wide)
    diag = jnp.sum(jnp.where(sub == lan, wide, 0.0), axis=1, keepdims=True)
    inverse = wide[:, NPIV:] * lax.rsqrt(diag)
    basis_in = nn(inverse, spectra_in.astype(jnp.float32), HIGHEST)
    basis_own = nn(inverse, spectra_own, HIGHEST)
    cross = nt(basis_own[32:], basis_own[:32], HIGHEST)
    coef = jnp.concatenate(
        [basis_in[:32], basis_in[32:] - nn(cross, basis_in[:32], HIGHEST)], axis=0
    )
    remain = one(same, jnp.float32) - tn(coef, basis_own, HIGHEST)
    mh_ref[...], ml_ref[...] = split(remain)
    ch_ref[...], cl_ref[...] = split(coef)

    @pl.loop(0, NCH)
    def _(k):
        ck = chunk_at(k)
        pltpu.make_async_copy(sb.at[ck, z], p1.at[k, z], local_sem.at[k]).wait()
        pltpu.make_async_copy(p1.at[k, 0 : NZ - 1], p1.at[k, 0 : NZ - 1], z_recv.at[k]).wait()
        for zh in range(4):
            lines = jnp.concatenate([p1[k, zh * 4 + zl] for zl in range(4)], axis=1)
            moved = nn(lines, perm[...])
            for i in range(PER):
                for s in range(4):
                    stage[s, (i * 4 + zh) * 8 : (i * 4 + zh + 1) * 8, :] = (
                        moved[i * 8 : (i + 1) * 8, s * 128 : (s + 1) * 128]
                    )
        for i in range(PER):
            for c4 in range(4):
                for s in range(4):
                    rows = stage[s, pl.ds(i * 32 + c4, 8, stride=4), :]
                    tb[k, i, c4 * 4 + s] = rows.astype(jnp.bfloat16)

        for i in range(PER):
            qq = ck * PER + i

            @pl.when(qq != q)
            def _():
                pltpu.make_async_remote_copy(
                    tb.at[k, i], x_ref.at[:, q], q_send.at[0], q_recv.at[0],
                    device_id=q_device(qq), device_id_type=MESH,
                ).start()

            @pl.when(qq == q)
            def _():
                pltpu.make_async_copy(tb.at[k, i], x_ref.at[:, q], local_sem.at[NCH]).start()

    pltpu.make_async_copy(tb.at[0, 0], x_ref.at[:, q], local_sem.at[NCH]).wait()
    pltpu.make_async_copy(
        x_ref.at[:, 0 : NQ - 1], x_ref.at[:, 0 : NQ - 1], q_recv.at[0]
    ).wait()
    pltpu.make_async_copy(
        x_ref.at[:, 0 : NQ - 1], x_ref.at[:, 0 : NQ - 1], q_send.at[0]
    ).wait()
    pltpu.make_async_copy(p1.at[:, 0 : NZ - 1], p1.at[:, 0 : NZ - 1], z_send.at[0]).wait()
    pltpu.make_async_copy(pz.at[0 : NZ - 1], pz.at[0 : NZ - 1], pz_send.at[0]).wait()
    pltpu.make_async_copy(rs.at[0 : NQ - 1], rs.at[0 : NQ - 1], pq_send.at[0]).wait()


def project(x_ref, mh_ref, ml_ref, ch_ref, cl_ref, r_ref, c_ref):
    for c in range(x_ref.shape[0]):
        x = x_ref[c]
        r_ref[c] = (tn(x, mh_ref[...]) + tn(x, ml_ref[...])).astype(r_ref.dtype)
        c_ref[:, c, :] = (nn(ch_ref[...], x) + nn(cl_ref[...], x)).astype(c_ref.dtype)


def shards(band_images, pivots):
    vmem = pl.BlockSpec(memory_space=pltpu.VMEM)
    half = jnp.bfloat16
    dma = pltpu.SemaphoreType.DMA
    x, mh, ml, ch, cl = pl.pallas_call(
        exchange,
        out_shape=(
            jax.ShapeDtypeStruct((16, NQ, 8, 128), half),
            jax.ShapeDtypeStruct((BANDS, BANDS), half),
            jax.ShapeDtypeStruct((BANDS, BANDS), half),
            jax.ShapeDtypeStruct((NPIV, BANDS), half),
            jax.ShapeDtypeStruct((NPIV, BANDS), half),
        ),
        in_specs=[vmem, vmem],
        out_specs=(vmem,) * 5,
        scratch_shapes=[
            pltpu.VMEM((NCH, NZ, PER * 8, 128), half),
            pltpu.VMEM((NCH, NZ, PER * 8, 128), half),
            pltpu.VMEM((NCH, PER, 16, 8, 128), half),
            pltpu.VMEM((4, PER * 32, 128), jnp.float32),
            pltpu.VMEM((512, 512), half),
            pltpu.VMEM((8, 128), half),
            pltpu.VMEM((NZ, 8, 128), half),
            pltpu.VMEM((8, 128), half),
            pltpu.VMEM((NQ, 8, 128), half),
            dma((NCH + 1,)), dma((1,)), dma((NCH,)), dma((1,)), dma((1,)),
            dma((1,)), dma((1,)), dma((1,)), dma((1,)),
        ],
        compiler_params=pltpu.CompilerParams(
            collective_id=0, has_side_effects=True, vmem_limit_bytes=32 << 20
        ),
        name="exchange",
    )(band_images, pivots)
    whole = lambda *shape: pl.BlockSpec(shape, lambda i: (0,) * len(shape))
    return pl.pallas_call(
        project,
        grid=(2,),
        out_shape=(
            jax.ShapeDtypeStruct((16, 128, BANDS), half),
            jax.ShapeDtypeStruct((NPIV, 16, 128), half),
        ),
        in_specs=[
            pl.BlockSpec((8, BANDS, 128), lambda i: (i, 0, 0)),
            whole(BANDS, BANDS), whole(BANDS, BANDS), whole(NPIV, BANDS), whole(NPIV, BANDS),
        ],
        out_specs=(
            pl.BlockSpec((8, 128, BANDS), lambda i: (i, 0, 0)),
            pl.BlockSpec((NPIV, 8, 128), lambda i: (0, i, 0)),
        ),
        compiler_params=pltpu.CompilerParams(vmem_limit_bytes=24 << 20),
        name="project",
    )(x.reshape(16, BANDS, 128), mh, ml, ch, cl)


def solution(mesh):
    return jax.shard_map(
        shards,
        mesh=mesh,
        in_specs=(P("pix", "row", None), P()),
        out_specs=(P(("pix", "row"), None, None), P(None, ("pix", "row"), None)),
        check_vma=False,
    )
```

time: 626 us -> 74.6 us (0.12)
  waiting for transfers between devices: 433 us -> 0 us
  blocking collectives: 76.3 us -> 0 us
  Pallas kernels: 0 us -> 71.9 us
  local copies, waits for them, and re-layouts: 71.7 us -> 1.9 us
  between operations: 14.2 us -> 0.65 us
  other arithmetic: 12.2 us -> 0 us
  matrix products: 9.88 us -> 0 us
  starting transfers between devices: 8.26 us -> 0 us
    psum x1 -> x0, waiting for transfers between devices: 433 us -> none  [shards(): spectra = lax.psum(placed, ('pix', 'row'))]
    all_to_all x1 -> x0, blocking collectives: 76.3 us -> none  [shards(): lax.all_to_all(shaped, 'pix', split_axis=2, concat_axis=0, tiled=True)]
    pallas_call x0 -> x2, Pallas kernels: none -> 71.9 us  [the longest x1 69.6 us: shards(): pl.pallas_call(exchange, out_shape=(jax.ShapeDtypeStruct((16, NQ, 8, 128)...]
    unnamed x11 -> x4, local copies, waits for them, and re-layouts: 56.5 us -> 1.9 us
    another operation x5 -> x0, other arithmetic: 12.1 us -> none  [the longest x3 6.52 us: orthonormal(): factor = jnp.linalg.cholesky(gram)]
    dot_general x5 -> x0, matrix products: 8.77 us -> none  [the longest x1 2.81 us: project(): jnp.einsum('kcl,kb->clb', coef_two, second, precision=highest)]
    all_to_all x1 -> x0, starting transfers between devices: 8.26 us -> none  [shards(): lax.all_to_all(lax.all_to_all(shaped, 'pix', split_axis=2, concat_axis=0,...]
    all_to_all x2 -> x0, local copies, waits for them, and re-layouts: 7.28 us -> none  [the longest x1 6.94 us: shards(): lax.all_to_all(shaped, 'pix', split_axis=2, concat_axis=0, tiled=True)]
  transfers between devices with their start and end apart: 2 -> 0, of which waited for: 1 -> 0; matrix products, arithmetic and copies ran while one was open for 9% -> 0% of each run, Pallas kernels for 0% -> 0%
where the time goes in v1:
time: 74.6 us; the launch traced here: 74.5 us
  Pallas kernels  71.9 us (96%)
  local copies, waits for them, and re-layouts  1.9 us (3%)
    pallas_call x1, Pallas kernels, shards(): pl.pallas_call(exchange, out_shape=(jax.ShapeDtypeStruct((16, NQ, 8, 128)...  69.6 us
    pallas_call x1, Pallas kernels, shards(): pl.pallas_call(project, grid=(2,), out_shape=(jax.ShapeDtypeStruct((16, 1...  2.32 us
    unnamed x4, local copies, waits for them, and re-layouts  1.9 us

profile of v1, /device:TPU:1, one launch (start us, length us, event | category | flops | bytes accessed | tf_op | source)
XLA Modules:
  0.0 74.5 jit_solution(11409560640667036761)
XLA Ops:
  0.6 0.0 copy-start
  0.6 1.2 %copy-done = bf16[2,32,8192]{2,1,0:T(8,128)(2,1)S(1)} copy-done((bf16[2,32,8192]{2,1,0:T(8,128)(2,1)S(1)}, bf16[2,32,8192]{2,1,0:T(8,128)(2,1)}, u32[]{:S(2)}) %copy-start) | copy-done | bytes 1048600
  1.9 0.0 copy-start.1
  1.9 0.7 copy-done.1
  2.5 69.6 %exchange.1 = (bf16[16,32,8,128]{3,2,1,0:T(8,128)(2,1)S(1)}, bf16[256,256]{1,0:T(8,128)(2,1)S(1)}, bf16[256,256]{1,0:T(8,128)(2,1)S(1)}, bf16[64,256]{1,0:T(8,128)(2,1)S(1)}, bf16[64,256]{1,0:T(8,128)(2,1)S(1)}) custom-call(bf16[2,32,8192]{2,1,0:T(8,128)(2,1)S(1)} %copy-done, s32[2,32]{1,0:T(2,128)S(1)} %copy-done.1), custom_call_target="tpu_custom_call" | custom-call | tf_op jit(solution)/shard_map/exchange/pallas_call | solution.py:285
  72.1 2.3 %project.1 = (bf16[16,128,256]{2,1,0:T(8,128)(2,1)}, bf16[64,16,128]{2,1,0:T(8,128)(2,1)}) custom-call(bf16[16,256,128]{2,1,0:T(8,128)(2,1)S(1)} %bitcast.1, bf16[256,256]{1,0:T(8,128)(2,1)S(1)} %get-tuple-element.8.mh_ref, bf16[256,256]{1,0:T(8,128)(2,1)S(1)} %get-tuple-element.9.ml_ref, bf16[64,256]{1,0:T(8,128)(2,1)S(1)} %get-tuple-element.10.ch_ref, ...), custom_call_target="tpu_custom_call" | custom-call | tf_op jit(solution)/shard_map/project/pallas_call | solution.py:315
Async XLA Ops:
  0.6 1.2 %copy-start = (bf16[2,32,8192]{2,1,0:T(8,128)(2,1)S(1)}, bf16[2,32,8192]{2,1,0:T(8,128)(2,1)}, u32[]{:S(2)}) copy-start(bf16[2,32,8192]{2,1,0:T(8,128)(2,1)} %a_ref.1) | copy-start | bytes 3145732
  1.9 0.7 copy-start.1

commit v2 on v1

--- a/solution.py
+++ b/solution.py
@@ -13,9 +13,10 @@
 NQ = 32
 NPIV = 64
 BANDS = 256
-NCH = 8
-PER = NQ // NCH
-SUB = 16 // NCH
+SIZES = (4, 4, 4)
+CHIPS = 16 - sum(SIZES)
+STARTS = tuple(sum(SIZES[:k]) for k in range(len(SIZES)))
+NCH = len(SIZES)
 
 
 def iota(shape, dim):
@@ -53,17 +54,17 @@
 
 
 def exchange(
-    a_ref, piv_ref,
+    a_hbm, piv_hbm,
     x_ref, mh_ref, ml_ref, ch_ref, cl_ref,
-    sb, p1, tb, stage, perm, ps, pz, pq, rs,
-    local_sem, z_send, z_recv, q_send, q_recv, pz_send, pz_recv, pq_send, pq_recv,
+    a_ref, piv_ref, sb, p1, last, crossed, landed, tb, stage, perm, ps, pz, pq, rs,
+    in_sem, local_sem, z_send, z_recv, c_send, c_recv, l_send, l_recv, q_send, q_recv, pz_send, pz_recv, pq_send, pq_recv,
 ):
     pix = lax.axis_index("pix")
     row = lax.axis_index("row")
     q = lax.rem(pix, NQ)
     z_hi = pix // NQ
     z = z_hi * 4 + row
-    own_chunk = q // PER
+    own_chip = q // 2
 
     def z_device(zz):
         return ((zz // 4) * NQ + q, lax.rem(zz, 4))
@@ -71,6 +72,10 @@
     def q_device(qq):
         return (z_hi * NQ + qq, row)
 
+    load_a = pltpu.make_async_copy(a_hbm, a_ref, in_sem.at[0])
+    load_a.start()
+    load_piv = pltpu.make_async_copy(piv_hbm, piv_ref, in_sem.at[1])
+    load_piv.start()
     barrier = pltpu.get_barrier_semaphore()
 
     @pl.loop(1, NZ)
@@ -94,36 +99,90 @@
     lane = iota((32, 128), 1)
     masks = [one((lane & 3) == s) for s in range(4)]
 
-    def chunk_at(k):
-        return lax.rem(own_chunk + 1 + k, NCH)
-
-    def relayout(ck):
-        for i in range(SUB):
-            for zh in range(4):
-                col = pl.multiple_of((zh * 16 + ck * SUB + i) * 128, 128)
-                halves = []
-                for j in range(2):
-                    a = a_ref[j, :, pl.ds(col, 128)]
-                    halves.append(jnp.concatenate([a * m for m in masks], axis=0))
-                out = nt(pick, jnp.concatenate(halves, axis=1)).astype(jnp.bfloat16)
-                for m in range(8):
-                    sb[ck, zh * 4 + m % 4, (i * 2 + m // 4) * 8 : (i * 2 + m // 4 + 1) * 8, :] = (
-                        out[m * 8 : (m + 1) * 8, :]
-                    )
-
-    def send_z(k, ck):
-        pltpu.make_async_copy(sb.at[ck, z], p1.at[k, z], local_sem.at[k]).start()
+    def chip_at(r):
+        return lax.rem(own_chip + 1 + r, 16)
+
+    def tiles(r, store):
+        chip = chip_at(r)
+        for zh in range(4):
+            col = pl.multiple_of((zh * 16 + chip) * 128, 128)
+            halves = []
+            for j in range(2):
+                a = a_ref[j, :, pl.ds(col, 128)]
+                halves.append(jnp.concatenate([a * m for m in masks], axis=0))
+            out = nt(pick, jnp.concatenate(halves, axis=1)).astype(jnp.bfloat16)
+            for m in range(8):
+                store(zh * 4 + m % 4, m // 4, out[m * 8 : (m + 1) * 8, :])
+
+    def relayout(k):
+        @pl.loop(STARTS[k], STARTS[k] + SIZES[k])
+        def _(r):
+            def store(zz, core, tile):
+                sb[zz, r, core * 8 : (core + 1) * 8, :] = tile
+
+            tiles(r, store)
+
+    def relayout_last():
+        @pl.loop(0, CHIPS)
+        def _(r):
+            def store(zz, core, tile):
+                last[r, core, zz] = tile
+
+            tiles(r + 16 - CHIPS, store)
+
+    def cross():
+        for r in range(CHIPS):
+            for core in range(2):
+                qq = chip_at(r + 16 - CHIPS) * 2 + core
+                slot = r * 2 + lax.rem(q, 2)
+
+                @pl.when(qq != q)
+                def _():
+                    pltpu.make_async_remote_copy(
+                        last.at[r, core], crossed.at[slot], c_send.at[0], c_recv.at[0],
+                        device_id=q_device(qq), device_id_type=MESH,
+                    ).start()
+
+                @pl.when(qq == q)
+                def _():
+                    pltpu.make_async_copy(
+                        last.at[r, core], crossed.at[slot], local_sem.at[NCH + 1]
+                    ).start()
+
+    def send_last():
+        pltpu.make_async_copy(last.at[0, 0], crossed.at[0], local_sem.at[NCH + 1]).wait()
+        others = 2 * CHIPS - 1
+        pltpu.make_async_copy(
+            crossed.at[0:others], crossed.at[0:others], c_recv.at[0]
+        ).wait()
+        pltpu.make_async_copy(crossed.at[:, z], landed.at[z], local_sem.at[NCH + 1]).start()
 
         @pl.loop(0, NZ - 1)
         def _(i):
             zz = lax.rem(z + far_order(i), NZ)
             pltpu.make_async_remote_copy(
-                sb.at[ck, zz], p1.at[k, z], z_send.at[0], z_recv.at[k],
+                crossed.at[:, zz], landed.at[z], l_send.at[0], l_recv.at[0],
                 device_id=z_device(zz), device_id_type=MESH,
             ).start()
 
-    relayout(chunk_at(0))
-
+    def send_z(k):
+        part = pl.ds(STARTS[k], SIZES[k])
+        pltpu.make_async_copy(sb.at[z, part], p1.at[z, part], local_sem.at[k]).start()
+
+        @pl.loop(0, NZ - 1)
+        def _(i):
+            zz = lax.rem(z + far_order(i), NZ)
+            pltpu.make_async_remote_copy(
+                sb.at[zz, part], p1.at[z, part], z_send.at[0], z_recv.at[k],
+                device_id=z_device(zz), device_id_type=MESH,
+            ).start()
+
+    load_a.wait()
+    relayout(0)
+    pl.semaphore_wait(barrier, NZ - 1 + NQ - 1)
+    send_z(0)
+
+    load_piv.wait()
     pivots = jnp.concatenate([piv_ref[0:1, :], piv_ref[1:2, :]], axis=1)
     column = pivots & 8191
     offset = (pivots >> 13) - row * 32
@@ -147,8 +206,6 @@
     tile = jnp.where(rows8 == 0, own[0], jnp.where(rows8 == 1, own[1], 0.0))
     ps[...] = jnp.concatenate([tile, jnp.zeros_like(tile)], axis=1).astype(jnp.bfloat16)
 
-    pl.semaphore_wait(barrier, NZ - 1 + NQ - 1)
-
     pltpu.make_async_copy(ps, pz.at[z], local_sem.at[NCH]).start()
 
     @pl.loop(0, NZ - 1)
@@ -159,13 +216,13 @@
             device_id=z_device(zz), device_id_type=MESH,
         ).start()
 
-    send_z(0, chunk_at(0))
-
-    @pl.loop(1, NCH)
-    def _(k):
-        ck = chunk_at(k)
-        relayout(ck)
-        send_z(k, ck)
+
+    relayout_last()
+    cross()
+    for k in range(1, NCH):
+        relayout(k)
+        send_z(k)
+    send_last()
 
     pltpu.make_async_copy(ps, pz.at[z], local_sem.at[NCH]).wait()
     pltpu.make_async_copy(pz.at[0 : NZ - 1], pz.at[0 : NZ - 1], pz_recv.at[0]).wait()
@@ -226,47 +283,63 @@
     mh_ref[...], ml_ref[...] = split(remain)
     ch_ref[...], cl_ref[...] = split(coef)
 
-    @pl.loop(0, NCH)
-    def _(k):
-        ck = chunk_at(k)
-        pltpu.make_async_copy(sb.at[ck, z], p1.at[k, z], local_sem.at[k]).wait()
-        pltpu.make_async_copy(p1.at[k, 0 : NZ - 1], p1.at[k, 0 : NZ - 1], z_recv.at[k]).wait()
+    def regroup(count, load, store):
         for zh in range(4):
-            lines = jnp.concatenate([p1[k, zh * 4 + zl] for zl in range(4)], axis=1)
+            lines = jnp.concatenate([load(zh * 4 + zl) for zl in range(4)], axis=1)
             moved = nn(lines, perm[...])
-            for i in range(PER):
+            for i in range(count):
                 for s in range(4):
                     stage[s, (i * 4 + zh) * 8 : (i * 4 + zh + 1) * 8, :] = (
                         moved[i * 8 : (i + 1) * 8, s * 128 : (s + 1) * 128]
                     )
-        for i in range(PER):
+        for i in range(count):
             for c4 in range(4):
                 for s in range(4):
                     rows = stage[s, pl.ds(i * 32 + c4, 8, stride=4), :]
-                    tb[k, i, c4 * 4 + s] = rows.astype(jnp.bfloat16)
-
-        for i in range(PER):
-            qq = ck * PER + i
-
-            @pl.when(qq != q)
-            def _():
-                pltpu.make_async_remote_copy(
-                    tb.at[k, i], x_ref.at[:, q], q_send.at[0], q_recv.at[0],
-                    device_id=q_device(qq), device_id_type=MESH,
-                ).start()
-
-            @pl.when(qq == q)
-            def _():
-                pltpu.make_async_copy(tb.at[k, i], x_ref.at[:, q], local_sem.at[NCH]).start()
-
-    pltpu.make_async_copy(tb.at[0, 0], x_ref.at[:, q], local_sem.at[NCH]).wait()
-    pltpu.make_async_copy(
-        x_ref.at[:, 0 : NQ - 1], x_ref.at[:, 0 : NQ - 1], q_recv.at[0]
-    ).wait()
-    pltpu.make_async_copy(
-        x_ref.at[:, 0 : NQ - 1], x_ref.at[:, 0 : NQ - 1], q_send.at[0]
-    ).wait()
-    pltpu.make_async_copy(p1.at[:, 0 : NZ - 1], p1.at[:, 0 : NZ - 1], z_send.at[0]).wait()
+                    store(i, c4 * 4 + s, rows.astype(jnp.bfloat16))
+
+    for k in range(NCH):
+        start, size = STARTS[k], SIZES[k]
+        part = pl.ds(start, size)
+        pltpu.make_async_copy(sb.at[z, part], p1.at[z, part], local_sem.at[k]).wait()
+        pltpu.make_async_copy(
+            p1.at[0 : NZ - 1, part], p1.at[0 : NZ - 1, part], z_recv.at[k]
+        ).wait()
+
+        def load(zz):
+            return p1[zz, start : start + size].reshape(size * 16, 128)
+
+        def store(i, c, tile):
+            tb[start * 2 + i, c] = tile
+
+        regroup(size * 2, load, store)
+        for i in range(size * 2):
+            pltpu.make_async_remote_copy(
+                tb.at[start * 2 + i], x_ref.at[:, q], q_send.at[0], q_recv.at[0],
+                device_id=q_device(chip_at(start + i // 2) * 2 + i % 2), device_id_type=MESH,
+            ).start()
+
+    pltpu.make_async_copy(crossed.at[:, z], landed.at[z], local_sem.at[NCH + 1]).wait()
+    pltpu.make_async_copy(landed.at[0 : NZ - 1], landed.at[0 : NZ - 1], l_recv.at[0]).wait()
+    sources = [
+        lax.rem(own_chip + 31 - (r + 16 - CHIPS), 16) * 2 + core
+        for r in range(CHIPS) for core in range(2)
+    ]
+
+    def load_landed(zz):
+        return landed[zz].reshape(CHIPS * 16, 128)
+
+    def store_landed(i, c, tile):
+        x_ref[c, sources[i]] = tile
+
+    regroup(CHIPS * 2, load_landed, store_landed)
+    far = 2 * sum(SIZES)
+    pltpu.make_async_copy(x_ref.at[:, 0:far], x_ref.at[:, 0:far], q_recv.at[0]).wait()
+    pltpu.make_async_copy(x_ref.at[:, 0:far], x_ref.at[:, 0:far], q_send.at[0]).wait()
+    others = 2 * CHIPS - 1
+    pltpu.make_async_copy(crossed.at[0:others], crossed.at[0:others], c_send.at[0]).wait()
+    pltpu.make_async_copy(landed.at[0 : NZ - 1], landed.at[0 : NZ - 1], l_send.at[0]).wait()
+    pltpu.make_async_copy(p1.at[0 : NZ - 1], p1.at[0 : NZ - 1], z_send.at[0]).wait()
     pltpu.make_async_copy(pz.at[0 : NZ - 1], pz.at[0 : NZ - 1], pz_send.at[0]).wait()
     pltpu.make_async_copy(rs.at[0 : NQ - 1], rs.at[0 : NQ - 1], pq_send.at[0]).wait()
 
@@ -291,26 +364,35 @@
             jax.ShapeDtypeStruct((NPIV, BANDS), half),
             jax.ShapeDtypeStruct((NPIV, BANDS), half),
         ),
-        in_specs=[vmem, vmem],
+        in_specs=[pl.BlockSpec(memory_space=pltpu.HBM)] * 2,
         out_specs=(vmem,) * 5,
         scratch_shapes=[
-            pltpu.VMEM((NCH, NZ, PER * 8, 128), half),
-            pltpu.VMEM((NCH, NZ, PER * 8, 128), half),
-            pltpu.VMEM((NCH, PER, 16, 8, 128), half),
-            pltpu.VMEM((4, PER * 32, 128), jnp.float32),
+            pltpu.VMEM(band_images.shape, half),
+            pltpu.VMEM(pivots.shape, jnp.int32),
+            pltpu.VMEM((NZ, 16 - CHIPS, 16, 128), half),
+            pltpu.VMEM((NZ, 16 - CHIPS, 16, 128), half),
+            pltpu.VMEM((CHIPS, 2, NZ, 8, 128), half),
+            pltpu.VMEM((2 * CHIPS, NZ, 8, 128), half),
+            pltpu.VMEM((NZ, 2 * CHIPS, 8, 128), half),
+            pltpu.VMEM((2 * (16 - CHIPS), 16, 8, 128), half),
+            pltpu.VMEM((4, max(*SIZES, CHIPS) * 64, 128), jnp.float32),
             pltpu.VMEM((512, 512), half),
             pltpu.VMEM((8, 128), half),
             pltpu.VMEM((NZ, 8, 128), half),
             pltpu.VMEM((8, 128), half),
             pltpu.VMEM((NQ, 8, 128), half),
-            dma((NCH + 1,)), dma((1,)), dma((NCH,)), dma((1,)), dma((1,)),
+            dma((2,)), dma((NCH + 2,)), dma((1,)), dma((NCH,)), dma((1,)), dma((1,)),
+            dma((1,)), dma((1,)), dma((1,)), dma((1,)),
             dma((1,)), dma((1,)), dma((1,)), dma((1,)),
         ],
         compiler_params=pltpu.CompilerParams(
             collective_id=0, has_side_effects=True, vmem_limit_bytes=32 << 20
         ),
         name="exchange",
-    )(band_images, pivots)
+    )(
+        pltpu.with_memory_space_constraint(band_images, pltpu.HBM),
+        pltpu.with_memory_space_constraint(pivots, pltpu.HBM),
+    )
     whole = lambda *shape: pl.BlockSpec(shape, lambda i: (0,) * len(shape))
     return pl.pallas_call(
         project,

time: 74.6 us -> 67.2 us (0.901)
  Pallas kernels: 71.9 us -> 66.5 us
  local copies, waits for them, and re-layouts: 1.9 us -> 0 us
    pallas_call x1, Pallas kernels: 69.6 us -> 64.2 us  [shards(): pl.pallas_call(exchange, out_shape=(jax.ShapeDtypeStruct((16, NQ, 8, 128)...]
    unnamed x4 -> x0, local copies, waits for them, and re-layouts: 1.9 us -> none
where the time goes in v2:
time: 67.2 us; the launch traced here: 67.1 us
  Pallas kernels  66.5 us (99%)
    pallas_call x1, Pallas kernels, shards(): pl.pallas_call(exchange, out_shape=(jax.ShapeDtypeStruct((16, NQ, 8, 128)...  64.2 us
    pallas_call x1, Pallas kernels, shards(): pl.pallas_call(project, grid=(2,), out_shape=(jax.ShapeDtypeStruct((16, 1...  2.27 us

profile of v2, /device:TPU:1, one launch (start us, length us, event | category | flops | bytes accessed | tf_op | source)
XLA Modules:
  0.0 67.1 jit_solution(5774550733723286605)
XLA Ops:
  0.6 64.2 %exchange.1 = (bf16[16,32,8,128]{3,2,1,0:T(8,128)(2,1)S(1)}, bf16[256,256]{1,0:T(8,128)(2,1)S(1)}, bf16[256,256]{1,0:T(8,128)(2,1)S(1)}, bf16[64,256]{1,0:T(8,128)(2,1)S(1)}, bf16[64,256]{1,0:T(8,128)(2,1)S(1)}) custom-call(bf16[2,32,8192]{2,1,0:T(8,128)(2,1)} %a_hbm.1, s32[2,32]{1,0:T(2,128)} %piv_hbm.1), custom_call_target="tpu_custom_call" | custom-call | tf_op jit(solution)/shard_map/exchange/pallas_call | solution.py:358
  64.8 2.3 %project.1 = (bf16[16,128,256]{2,1,0:T(8,128)(2,1)}, bf16[64,16,128]{2,1,0:T(8,128)(2,1)}) custom-call(bf16[16,256,128]{2,1,0:T(8,128)(2,1)S(1)} %bitcast.1, bf16[256,256]{1,0:T(8,128)(2,1)S(1)} %get-tuple-element.8.mh_ref, bf16[256,256]{1,0:T(8,128)(2,1)S(1)} %get-tuple-element.9.ml_ref, bf16[64,256]{1,0:T(8,128)(2,1)S(1)} %get-tuple-element.10.ch_ref, ...), custom_call_target="tpu_custom_call" | custom-call | tf_op jit(solution)/shard_map/project/pallas_call | solution.py:397

commit v3 on v2

--- a/solution.py
+++ b/solution.py
@@ -50,12 +50,12 @@
 
 def far_order(i):
     half = (i + 1) // 2
-    return jnp.where(lax.rem(i, 2) == 1, 8 - half, 8 + half)
+    return jnp.where(lax.rem(i, 2) == lax.rem(lax.axis_index("pix"), 2), 8 - half, 8 + half)
 
 
 def exchange(
     a_hbm, piv_hbm,
-    x_ref, mh_ref, ml_ref, ch_ref, cl_ref,
+    x_ref, m_ref, c_ref,
     a_ref, piv_ref, sb, p1, last, crossed, landed, tb, stage, perm, ps, pz, pq, rs,
     in_sem, local_sem, z_send, z_recv, c_send, c_recv, l_send, l_recv, q_send, q_recv, pz_send, pz_recv, pq_send, pq_recv,
 ):
@@ -139,29 +139,29 @@
                 @pl.when(qq != q)
                 def _():
                     pltpu.make_async_remote_copy(
-                        last.at[r, core], crossed.at[slot], c_send.at[0], c_recv.at[0],
+                        last.at[r, core], crossed.at[:, slot], c_send.at[0], c_recv.at[0],
                         device_id=q_device(qq), device_id_type=MESH,
                     ).start()
 
                 @pl.when(qq == q)
                 def _():
                     pltpu.make_async_copy(
-                        last.at[r, core], crossed.at[slot], local_sem.at[NCH + 1]
+                        last.at[r, core], crossed.at[:, slot], local_sem.at[NCH + 1]
                     ).start()
 
     def send_last():
-        pltpu.make_async_copy(last.at[0, 0], crossed.at[0], local_sem.at[NCH + 1]).wait()
+        pltpu.make_async_copy(last.at[0, 0], crossed.at[:, 0], local_sem.at[NCH + 1]).wait()
         others = 2 * CHIPS - 1
         pltpu.make_async_copy(
-            crossed.at[0:others], crossed.at[0:others], c_recv.at[0]
+            crossed.at[:, 0:others], crossed.at[:, 0:others], c_recv.at[0]
         ).wait()
-        pltpu.make_async_copy(crossed.at[:, z], landed.at[z], local_sem.at[NCH + 1]).start()
+        pltpu.make_async_copy(crossed.at[z], landed.at[z], local_sem.at[NCH + 1]).start()
 
         @pl.loop(0, NZ - 1)
         def _(i):
             zz = lax.rem(z + far_order(i), NZ)
             pltpu.make_async_remote_copy(
-                crossed.at[:, zz], landed.at[z], l_send.at[0], l_recv.at[0],
+                crossed.at[zz], landed.at[z], l_send.at[0], l_recv.at[0],
                 device_id=z_device(zz), device_id_type=MESH,
             ).start()
 
@@ -280,8 +280,8 @@
         [basis_in[:32], basis_in[32:] - nn(cross, basis_in[:32], HIGHEST)], axis=0
     )
     remain = one(same, jnp.float32) - tn(coef, basis_own, HIGHEST)
-    mh_ref[...], ml_ref[...] = split(remain)
-    ch_ref[...], cl_ref[...] = split(coef)
+    m_ref[:BANDS, :], m_ref[BANDS:, :] = split(remain)
+    c_ref[:, :BANDS], c_ref[:, BANDS:] = split(coef)
 
     def regroup(count, load, store):
         for zh in range(4):
@@ -319,7 +319,7 @@
                 device_id=q_device(chip_at(start + i // 2) * 2 + i % 2), device_id_type=MESH,
             ).start()
 
-    pltpu.make_async_copy(crossed.at[:, z], landed.at[z], local_sem.at[NCH + 1]).wait()
+    pltpu.make_async_copy(crossed.at[z], landed.at[z], local_sem.at[NCH + 1]).wait()
     pltpu.make_async_copy(landed.at[0 : NZ - 1], landed.at[0 : NZ - 1], l_recv.at[0]).wait()
     sources = [
         lax.rem(own_chip + 31 - (r + 16 - CHIPS), 16) * 2 + core
@@ -337,45 +337,53 @@
     pltpu.make_async_copy(x_ref.at[:, 0:far], x_ref.at[:, 0:far], q_recv.at[0]).wait()
     pltpu.make_async_copy(x_ref.at[:, 0:far], x_ref.at[:, 0:far], q_send.at[0]).wait()
     others = 2 * CHIPS - 1
-    pltpu.make_async_copy(crossed.at[0:others], crossed.at[0:others], c_send.at[0]).wait()
+    pltpu.make_async_copy(crossed.at[:, 0:others], crossed.at[:, 0:others], c_send.at[0]).wait()
     pltpu.make_async_copy(landed.at[0 : NZ - 1], landed.at[0 : NZ - 1], l_send.at[0]).wait()
     pltpu.make_async_copy(p1.at[0 : NZ - 1], p1.at[0 : NZ - 1], z_send.at[0]).wait()
     pltpu.make_async_copy(pz.at[0 : NZ - 1], pz.at[0 : NZ - 1], pz_send.at[0]).wait()
     pltpu.make_async_copy(rs.at[0 : NQ - 1], rs.at[0 : NQ - 1], pq_send.at[0]).wait()
 
 
-def project(x_ref, mh_ref, ml_ref, ch_ref, cl_ref, r_ref, c_ref):
-    for c in range(x_ref.shape[0]):
+def project(x_ref, m_ref, w_ref, r_hbm, c_hbm, r_ref, c_ref, wide, sem):
+    copies = []
+    for c in range(16):
         x = x_ref[c]
-        r_ref[c] = (tn(x, mh_ref[...]) + tn(x, ml_ref[...])).astype(r_ref.dtype)
-        c_ref[:, c, :] = (nn(ch_ref[...], x) + nn(cl_ref[...], x)).astype(c_ref.dtype)
+        t = x.T
+        r_ref[c] = nn(jnp.concatenate([t, t], axis=1), m_ref[...]).astype(r_ref.dtype)
+        copies.append(pltpu.make_async_copy(r_ref.at[c], r_hbm.at[c], sem.at[c]))
+        copies[-1].start()
+        wide[c * NPIV : (c + 1) * NPIV, :] = nn(w_ref[...], jnp.concatenate([x, x], axis=0))
+    for k in range(NPIV):
+        c_ref[k] = wide[pl.ds(k, 16, stride=NPIV), :].astype(c_ref.dtype)
+    copies.append(pltpu.make_async_copy(c_ref, c_hbm, sem.at[16]))
+    copies[-1].start()
+    for copy in copies:
+        copy.wait()
 
 
 def shards(band_images, pivots):
     vmem = pl.BlockSpec(memory_space=pltpu.VMEM)
     half = jnp.bfloat16
     dma = pltpu.SemaphoreType.DMA
-    x, mh, ml, ch, cl = pl.pallas_call(
+    x, m, w = pl.pallas_call(
         exchange,
         out_shape=(
             jax.ShapeDtypeStruct((16, NQ, 8, 128), half),
-            jax.ShapeDtypeStruct((BANDS, BANDS), half),
-            jax.ShapeDtypeStruct((BANDS, BANDS), half),
-            jax.ShapeDtypeStruct((NPIV, BANDS), half),
-            jax.ShapeDtypeStruct((NPIV, BANDS), half),
+            jax.ShapeDtypeStruct((2 * BANDS, BANDS), half),
+            jax.ShapeDtypeStruct((NPIV, 2 * BANDS), half),
         ),
         in_specs=[pl.BlockSpec(memory_space=pltpu.HBM)] * 2,
-        out_specs=(vmem,) * 5,
+        out_specs=(vmem,) * 3,
         scratch_shapes=[
             pltpu.VMEM(band_images.shape, half),
             pltpu.VMEM(pivots.shape, jnp.int32),
             pltpu.VMEM((NZ, 16 - CHIPS, 16, 128), half),
             pltpu.VMEM((NZ, 16 - CHIPS, 16, 128), half),
             pltpu.VMEM((CHIPS, 2, NZ, 8, 128), half),
-            pltpu.VMEM((2 * CHIPS, NZ, 8, 128), half),
+            pltpu.VMEM((NZ, 2 * CHIPS, 8, 128), half),
             pltpu.VMEM((NZ, 2 * CHIPS, 8, 128), half),
             pltpu.VMEM((2 * (16 - CHIPS), 16, 8, 128), half),
-            pltpu.VMEM((4, max(*SIZES, CHIPS) * 64, 128), jnp.float32),
+            pltpu.VMEM((4, max(*SIZES, CHIPS) * 64 + 8, 128), jnp.float32),
             pltpu.VMEM((512, 512), half),
             pltpu.VMEM((8, 128), half),
             pltpu.VMEM((NZ, 8, 128), half),
@@ -393,25 +401,23 @@
         pltpu.with_memory_space_constraint(band_images, pltpu.HBM),
         pltpu.with_memory_space_constraint(pivots, pltpu.HBM),
     )
-    whole = lambda *shape: pl.BlockSpec(shape, lambda i: (0,) * len(shape))
     return pl.pallas_call(
         project,
-        grid=(2,),
         out_shape=(
             jax.ShapeDtypeStruct((16, 128, BANDS), half),
             jax.ShapeDtypeStruct((NPIV, 16, 128), half),
         ),
-        in_specs=[
-            pl.BlockSpec((8, BANDS, 128), lambda i: (i, 0, 0)),
-            whole(BANDS, BANDS), whole(BANDS, BANDS), whole(NPIV, BANDS), whole(NPIV, BANDS),
+        in_specs=[vmem] * 3,
+        out_specs=(pl.BlockSpec(memory_space=pltpu.HBM),) * 2,
+        scratch_shapes=[
+            pltpu.VMEM((16, 128, BANDS), half),
+            pltpu.VMEM((NPIV, 16, 128), half),
+            pltpu.VMEM((17 * NPIV, 128), jnp.float32),
+            dma((17,)),
         ],
-        out_specs=(
-            pl.BlockSpec((8, 128, BANDS), lambda i: (i, 0, 0)),
-            pl.BlockSpec((NPIV, 8, 128), lambda i: (0, i, 0)),
-        ),
         compiler_params=pltpu.CompilerParams(vmem_limit_bytes=24 << 20),
         name="project",
-    )(x.reshape(16, BANDS, 128), mh, ml, ch, cl)
+    )(x.reshape(16, BANDS, 128), m, w)
 
 
 def solution(mesh):

time: 67.2 us -> 67.2 us (level)
  no operation moved by 1% of the time
where the time goes in v3:
time: 67.2 us; the launch traced here: 67.1 us
  Pallas kernels  66.4 us (99%)
    pallas_call x1, Pallas kernels, shards(): pl.pallas_call(exchange, out_shape=(jax.ShapeDtypeStruct((16, NQ, 8, 128)...  64.2 us
    pallas_call x1, Pallas kernels, shards(): pl.pallas_call(project, out_shape=(jax.ShapeDtypeStruct((16, 128, BANDS),...  2.26 us

profile of v3, /device:TPU:1, one launch (start us, length us, event | category | flops | bytes accessed | tf_op | source)
XLA Modules:
  0.0 67.1 jit_solution(2788778525730355648)
XLA Ops:
  0.6 64.2 %exchange.1 = (bf16[16,32,8,128]{3,2,1,0:T(8,128)(2,1)S(1)}, bf16[512,256]{1,0:T(8,128)(2,1)S(1)}, bf16[64,512]{1,0:T(8,128)(2,1)S(1)}) custom-call(bf16[2,32,8192]{2,1,0:T(8,128)(2,1)} %a_hbm.1, s32[2,32]{1,0:T(2,128)} %piv_hbm.1), custom_call_target="tpu_custom_call" | custom-call | tf_op jit(solution)/shard_map/exchange/pallas_call | solution.py:368
  64.8 2.3 %project.1 = (bf16[16,128,256]{2,1,0:T(8,128)(2,1)}, bf16[64,16,128]{2,1,0:T(8,128)(2,1)}) custom-call(bf16[16,256,128]{2,1,0:T(8,128)(2,1)S(1)} %bitcast.1, bf16[512,256]{1,0:T(8,128)(2,1)S(1)} %get-tuple-element.6.m_ref, bf16[64,512]{1,0:T(8,128)(2,1)S(1)} %get-tuple-element.7.w_ref), custom_call_target="tpu_custom_call" | custom-call | tf_op jit(solution)/shard_map/project/pallas_call | solution.py:404
